TPU v7x, 32 devices: a whole 2x2x4 slice. The times are simulated.
32 devices in a mesh: dp: 8 (over z, x), mp: 4 (over y, core).
Axes of the slice: x: 2, y: 2, z: 4, core: 2. Of those that a mesh axis runs over, the one named last changes fastest.
Arguments:
- tokens: bfloat16 [16384, 512], P('dp'), may hold values from -6 to 6
- cotangent: bfloat16 [16384, 512], P('dp'), may hold values from -6 to 6
- bucket: int32 [16384, 1], P('dp'), may hold values from 0 to 7, as said below
- cell: int32 [16384], P('dp'), may hold values from 0 to 1, as said below
- features: bfloat16 [4, 64, 256], replicated, may hold values from -4 to 4
- qkv_weight: bfloat16 [3, 512, 512], P(None, None, 'mp'), may hold values from -0.25 to 0.25
- out_weight: bfloat16 [512, 512], P('mp'), may hold values from -1 to 1
- out_bias: float32 [512], replicated, may hold values from -3 to 3
- norm1_gain: float32 [512], replicated, may hold values from 0.25 to 1.75
- norm1_bias: float32 [512], replicated, may hold values from -3 to 3
- norm2_gain: float32 [512], replicated, may hold values from 0.25 to 1.75
- norm2_bias: float32 [512], replicated, may hold values from -3 to 3
- up_weight: bfloat16 [512, 2048], P(None, 'mp'), may hold values from -0.25 to 0.25
- up_bias: float32 [2048], P('mp'), may hold values from -3 to 3
- down_weight: bfloat16 [2048, 512], P('mp'), may hold values from -0.125 to 0.125
- down_bias: float32 [512], replicated, may hold values from -3 to 3
Outputs:
- output: bfloat16 [16384, 512], P('dp')
- grad_tokens: float32 [16384, 512], P('dp')
- grad_qkv_weight: float32 [3, 512, 512], P(None, None, 'mp')
- grad_out_weight: float32 [512, 512], P('mp')
- grad_out_bias: float32 [512], replicated
- grad_norm1_gain: float32 [512], replicated
- grad_norm1_bias: float32 [512], replicated
- grad_norm2_gain: float32 [512], replicated
- grad_norm2_bias: float32 [512], replicated
- grad_up_weight: float32 [512, 2048], P(None, 'mp')
- grad_up_bias: float32 [2048], P('mp')
- grad_down_weight: float32 [2048, 512], P('mp')
- grad_down_bias: float32 [512], replicated
Inputs may be any that keep to these rules, and one draw needn't show every extreme that they name: The 2048 rows of one device name every bucket at least once and one bucket at most 512 times, and every device names some bucket exactly 512 times. In every bucket one cell, drawn from the seed, holds tokens from every device.
All inputs are finite; a program needn't handle non-finite values.
Results may differ from a plain program's by a relative error of at most 0.012.
The roundings to bfloat16 on the way count: a program that leaves them out, or rounds other values in their place, can miss the bound.
Values may be sent and summed in bfloat16 or wider, within the bound.
A program may use at most 192 MiB of HBM per device.

v0:
```python
import functools
from types import SimpleNamespace

import jax
import jax.numpy as jnp
from jax import lax
from jax.experimental import pallas as pl
from jax.experimental.pallas import tpu as pltpu
from jax.sharding import PartitionSpec as P

HD = 64
FEATS = 4
STEP = 5
SEG = 2
PAD = 8
SCALE = HD**-0.25
HALF_SQUARE = 0.5 * SCALE * SCALE
EPS = 1e-05

BF = jnp.bfloat16
F32 = jnp.float32
MESH = pl.DeviceIdType.MESH
LANES = 128
TILE = 256


def dot(a, b):
    return jnp.dot(a, b, preferred_element_type=F32)


def dot_nt(a, b):
    return lax.dot_general(a, b, (((1,), (1,)), ((), ())), preferred_element_type=F32)


def dot_tn(a, b):
    return lax.dot_general(a, b, (((0,), (0,)), ((), ())), preferred_element_type=F32)


def lane(shape):
    return lax.broadcasted_iota(jnp.int32, shape, len(shape) - 1)


def roll_half(x):
    return pltpu.roll(x, HD, 1)


def loop(count, body, unroll=False):
    if unroll or count <= 3:
        for i in range(count):
            body(i)
    else:

        def step(i, carry):
            body(i)
            return carry

        lax.fori_loop(0, count, step, 0)


def rows_of(i, size):
    if isinstance(i, int):
        return pl.ds(i * size, size)
    return pl.ds(pl.multiple_of(i * size, size), size)


def normalised(values):
    average = jnp.mean(values, -1, keepdims=True)
    centred = values - average
    spread = jnp.mean(centred * centred, -1, keepdims=True)
    scale = lax.rsqrt(spread + EPS)
    return centred * scale, scale


def norm_back(upstream, hat, scale, gain):
    e = gain * upstream
    return (
        e
        - jnp.mean(e, -1, keepdims=True)
        - hat * jnp.mean(e * hat, -1, keepdims=True)
    ) * scale


def round_up(a, b):
    return (a + b - 1) // b * b


class Plan:
    def __init__(self, n, nm, tokens, width, local, feats, hidden):
        self.n, self.nm, self.T, self.D, self.L, self.M, self.F = (
            n,
            nm,
            tokens,
            width,
            local,
            feats,
            hidden,
        )
        self.H = local // HD
        self.HM = self.H * feats
        self.Tm = tokens // nm
        self.big = n > 8
        self.G8 = n * PAD
        self.rest = hidden + local
        self.tail = self.rest + width * local // width
        self.ru, self.rd, self.rk = (
            round_up((rows + n - 1) // n, 16) for rows in (width, self.tail, 2 * width)
        )
        self.per = self.Tm // TILE
        n2 = n // 2
        T, D, L, HM, Tm = self.T, self.D, self.L, self.HM, self.Tm
        vm = "vmem"
        states = (n, HM, SEG * HD)
        place = "hbm" if self.big else vm
        self.inputs = [
            ("tok", "hbm"),
            ("bkt", vm),
            ("cel", vm),
            ("feat", vm),
            ("wqkv", vm),
            ("g1", vm),
            ("b1", vm),
            ("ob", vm),
            ("g2", vm),
            ("b2", vm),
            ("db", vm),
            ("cot", "hbm"),
            ("ow", "hbm"),
            ("up", "hbm"),
            ("ub", "hbm"),
            ("dn", "hbm"),
        ]
        self.outputs = [
            ("out_o", "hbm", (T, D), BF),
            ("gtok_o", "hbm", (T, D), BF),
            ("upg_o", "hbm", (D, hidden), BF),
            ("dng_o", "hbm", (self.tail, D), BF),
            ("kvg_o", "hbm", (2 * D, L), BF),
            ("small_o", vm, (8, D), F32),
        ]
        big_states = [("sp", states), ("rb", states), ("sall", states), ("gall", states)]
        if self.big:
            self.outputs += [(name, "hbm", shape, BF) for name, shape in big_states]
        self.scratch = [
            ("wcat", (D, 4 * L), BF),
            ("f2", (L, HM), BF),
            ("wb", (HM, 2 * L), BF),
            ("ccb", (T, LANES), BF),
            ("oh2", (T, 2 * self.G8), BF),
            ("nm", (T, D), BF),
            ("qk", (2, T, L), BF),
            ("vv", (2, T, L), BF),
            ("qf", (T, HM), BF),
            ("kf", (T, HM), BF),
            ("ft", (HM, T), BF),
            ("tp", (n, PAD, LANES), F32),
            ("trb", (n, PAD, LANES), F32),
            ("tall", (n, PAD, LANES), F32),
            ("gtall", (n, PAD, LANES), F32),
            ("tot2", (2 * self.G8, HM), BF),
            ("acc", (HM, SEG * HD), F32),
            ("attf", (T, L), F32),
            ("inv", (T, L), F32),
            ("attb", (T, L), BF),
            ("arow", (nm, Tm, L), BF),
            ("wq_g", (nm, 3, D, L), BF),
            ("ow_g", (nm, L, D), BF),
            ("up_g", (nm, D, hidden), BF),
            ("ub_g", (nm, 1, hidden), F32),
            ("dn_g", (nm, hidden, D), BF),
            ("cotv", (Tm, D), BF),
            ("tokv", (Tm, D), BF),
            ("mid", (Tm, D), F32),
            ("nm2", (Tm, D), BF),
            ("act", (nm, Tm, hidden), BF),
            ("gp", (nm, Tm, hidden), BF),
            ("bo", (TILE, D), F32),
            ("gn2", (TILE, D), F32),
            ("gb", (Tm, D), BF),
            ("outv", (Tm, D), BF),
            ("small", (16, D), F32),
            ("small_m", (nm, 16, D), F32),
            ("small_d", (n, 8, D), F32),
            ("small_s", (8, D), F32),
            ("ends", (8, D), F32),
            ("last", (8, LANES), F32),
            ("last_m", (nm, 8, LANES), F32),
            ("last_d", (n, 8, LANES), F32),
            ("upp", (nm, D, hidden), BF),
            ("upc", (2, D, hidden), BF),
            ("upy", (n, self.ru, D), BF),
            ("upx", (n2, self.ru, D), BF),
            ("upz", (n2, self.ru, D), BF),
            ("dnp", (nm, self.rest, D), BF),
            ("dnc", (2, self.rest, D), BF),
            ("dny", (n, self.rd, D), BF),
            ("dnx", (n2, self.rd, D), BF),
            ("dnz", (n2, self.rd, D), BF),
            ("gar", (nm, Tm, L), BF),
            ("gad", (2, T, L), BF),
            ("gg", (2, T, L), BF),
            ("gd", (T, L), F32),
            ("grads", (3, T, L), BF),
            ("garr", (nm, 3, Tm, L), BF),
            ("kvp", (n, self.rk, L), BF),
            ("kvr", (n, self.rk, L), BF),
            ("kvl", (n, self.rk, L), BF),
        ]
        if self.big:
            self.scratch += [("stage_a", (2, HM, SEG * HD), BF), ("stage_b", (2, HM, SEG * HD), BF)]
        else:
            self.scratch += [(name, shape, BF) for name, shape in big_states]
            self.scratch += [("num", (T, LANES), F32), ("gkf", (T, self.M), F32)]
        self.sems = {
            **{name: n2 * self.H for name in ("rsx", "rsz", "agz", "agx", "gsx", "gsz", "ggz", "ggx")},
            **{name: n2 for name in ("rtx", "rtz", "atz", "atx", "gtx", "gtz", "hgz", "hgx")},
            **{name: nm * self.per for name in ("a2a", "gaa", "grk")},
            "grq": nm,
            "wy": 5,
            "wc": 10,
            "uc": 2,
            "uy": 1,
            "ux": n2,
            "uz": n2,
            "ugz": n2,
            "ugx": n2,
            "dc": 2,
            "dy": 1,
            "dx": n2,
            "dz": n2,
            "dgz": n2,
            "dgx": n2,
            "ks": n,
            "kg": n,
            "oy": 1,
            "oc": 2,
            "ty": self.per,
            "tc": 2 * self.per,
            "sm": nm,
            "sd": n,
            "lm": nm,
            "ld": n,
        }
        self.local_sems = 16

    def names(self):
        return (
            [x[0] for x in self.inputs]
            + [x[0] for x in self.outputs]
            + [x[0] for x in self.scratch]
            + [f"{k}_{end}" for k in self.sems for end in ("s", "r")]
            + ["lsem"]
        )


def layer_kernel(plan, *refs):
    r = SimpleNamespace(**dict(zip(plan.names(), refs, strict=True)))
    n, nm, T, D, L, M, HM, Tm, H = (
        plan.n,
        plan.nm,
        plan.T,
        plan.D,
        plan.L,
        plan.M,
        plan.HM,
        plan.Tm,
        plan.H,
    )
    hidden = plan.F
    n2 = n // 2
    tiles = T // TILE
    me, m = lax.axis_index("dp"), lax.axis_index("mp")
    sib = m + 1 - 2 * lax.rem(m, 2)
    far = lax.rem(m + nm // 2, nm)
    farsib = lax.rem(sib + nm // 2, nm)
    xpart = me + 1 - 2 * lax.rem(me, 2)
    xme, zme = lax.rem(me, 2), me // 2

    def sem(name, index):
        return getattr(r, f"{name}_s").at[index], getattr(r, f"{name}_r").at[index]

    def copy(src, dst, name, sent, dp=None, mp=None, got=None):
        send, _ = sem(name, sent)
        _, recv = sem(name, sent if got is None else got)
        return pltpu.make_async_remote_copy(
            src_ref=src,
            dst_ref=dst,
            send_sem=send,
            recv_sem=recv,
            device_id=(me if dp is None else dp, m if mp is None else mp),
            device_id_type=MESH,
        )

    def local(src, dst, index):
        return pltpu.make_async_copy(src, dst, r.lsem.at[index])

    low = lane((1, LANES)) < HD

    barrier = pltpu.get_barrier_semaphore()

    def greet(k):
        pl.semaphore_signal(
            barrier, inc=1, device_id=(lax.rem(me + 1 + k, n), m), device_id_type=MESH
        )

    loop(n - 1, greet)
    for k in range(1, nm):
        pl.semaphore_signal(
            barrier, inc=1, device_id=(me, lax.rem(m + k, nm)), device_id_type=MESH
        )

    mine = rows_of(m, Tm)
    tok_in = local(r.tok, r.nm, 10)
    own_in = [local(r.cot.at[mine], r.cotv, 0), local(r.tok.at[mine], r.tokv, 11)]
    for c in [tok_in, *own_in]:
        c.start()

    r.wcat[:, 0:L] = r.wqkv[0]
    r.wcat[:, L : 2 * L] = r.wqkv[1]
    wv = r.wqkv[2].astype(F32)
    wv_rolled = roll_half(wv)
    r.wcat[:, 2 * L : 3 * L] = jnp.where(low, wv, wv_rolled).astype(BF)
    r.wcat[:, 3 * L : 4 * L] = jnp.where(low, wv_rolled, wv).astype(BF)
    feature_rows = r.feat[STEP % FEATS]
    r.f2[...] = jnp.zeros((L, HM), BF)
    for h in range(H):
        r.f2[h * HD : (h + 1) * HD, h * M : (h + 1) * M] = feature_rows
    r.wb[:, 0:L] = r.f2[...].astype(F32).T.astype(BF)
    head_of_row = lax.broadcasted_iota(jnp.int32, (HM, L), 0) // M
    r.wb[:, L : 2 * L] = jnp.where(head_of_row == lane((HM, L)) // HD, 1.0, 0.0).astype(BF)

    count = T // LANES
    numbers = SEG * r.bkt[...].astype(F32) + r.cel[...].astype(F32)
    numbers = jnp.concatenate([numbers, jnp.zeros((LANES - count, LANES), F32)], 0).T
    for i in range(count):
        rows = pl.ds(i * LANES, LANES)
        column = jnp.broadcast_to(numbers[:, i : i + 1], (LANES, LANES))
        r.ccb[rows, :] = (column - jnp.where(low, 0.0, 1.0)).astype(BF)
        for block in range(2 * plan.G8 // LANES):
            place = (lane((1, LANES)) + block * LANES) % plan.G8
            number = place // PAD * SEG + place % SEG
            r.oh2[rows, block * LANES : (block + 1) * LANES] = jnp.where(
                column == number.astype(F32), 1.0, 0.0
            ).astype(BF)
    part_of_row = lax.broadcasted_iota(jnp.int32, (plan.G8, LANES), 0) % PAD // SEG

    def pack_totals(table):
        packed = jnp.zeros((plan.G8, LANES), F32)
        for q in range(HM // LANES):
            packed += jnp.where(part_of_row == q, table[:, q * LANES : (q + 1) * LANES], 0.0)
        return packed.reshape(n, PAD, LANES)

    def spread_totals(packed):
        packed = packed.reshape(plan.G8, LANES)
        return jnp.concatenate(
            [jnp.where(part_of_row == q, packed, 0.0) for q in range(HM // LANES)], 1
        )

    def phi(u):
        wide = u.astype(F32)
        squares = wide * wide
        first = jnp.sum(jnp.where(low, squares, 0.0), -1, keepdims=True)
        second = jnp.sum(jnp.where(low, 0.0, squares), -1, keepdims=True)
        projected = dot(u, r.f2[...]) * SCALE
        shift = jnp.where(lane((1, HM)) < M, first, second) * HALF_SQUARE
        return jnp.exp(projected - shift)

    tok_in.wait()
    pl.semaphore_wait(barrier, n - 1 + nm - 1)

    def project(i):
        rows = rows_of(i, TILE)
        hat, _ = normalised(r.nm[rows, :].astype(F32))
        normed = (hat * r.g1[...] + r.b1[...]).astype(BF)
        r.nm[rows, :] = normed
        u = dot(normed, r.wcat[:, L:]).astype(BF)
        k = u[:, 0:L]
        r.qk[1, rows, :] = k
        r.vv[0, rows, :], r.vv[1, rows, :] = u[:, L : 2 * L], u[:, 2 * L : 3 * L]
        features = phi(k)
        r.kf[rows, :] = features.astype(BF)
        r.ft[:, rows] = features.T.astype(BF)

    def queries(i):
        rows = rows_of(i, TILE)
        q = dot(r.nm[rows, :], r.wcat[:, 0:L]).astype(BF)
        r.qk[0, rows, :] = q
        r.qf[rows, :] = phi(q).astype(BF)

    shards = [
        (r.ow, r.ow_g),
        (r.up, r.up_g),
        (r.ub, r.ub_g),
        (r.dn, r.dn_g),
        (r.wqkv, r.wq_g),
    ]
    own_copies, y_copies, core_copies = [], [], []
    for i, (src, dst) in enumerate(shards):
        own_copies.append(local(src, dst.at[m], 1 + i))
        y_copies.append(copy(src, dst.at[m], "wy", i, mp=far))
        core_copies.append(copy(src, dst.at[m], "wc", 2 * i, mp=sib))
    for c in own_copies + y_copies + core_copies:
        c.start()
    loop(tiles, project)

    def state_pair(ref, p, stage):
        if plan.big:
            pltpu.sync_copy(ref.at[pl.ds(2 * p, 2)], stage)
            return stage
        return ref.at[pl.ds(2 * p, 2)]

    def masked_pair(rows, dup, p):
        code = r.ccb[rows, :]
        first = jnp.full((1, LANES), 1.0, F32) * (4 * p)
        left = jnp.where(code == first.astype(BF), dup, jnp.zeros_like(dup))
        right = jnp.where(code == (first + 2.0).astype(BF), dup, jnp.zeros_like(dup))
        return jnp.concatenate([left, right], 1)

    everything = pl.ds(0, T)

    def head_rows(h):
        return pl.ds(h * M, M)

    class States:
        def __init__(self, all_s, all_t, names):
            self.all_s, self.all_t = all_s, all_t
            self.x, self.tx, self.z, self.tz, self.gz, self.hz, self.gx, self.hx = names

        def both(self, h, state, totals):
            return [state, totals()] if h == 0 else [state]

        def to_x(self, p, h):
            j, hs = 2 * p + 1 - xme, head_rows(h)
            return self.both(
                h,
                copy(r.sp.at[j, hs], r.rb.at[p, hs], self.x, p * H + h, dp=xpart),
                lambda: copy(r.tp.at[j], r.trb.at[p], self.tx, p, dp=xpart),
            )

        def to_z(self, p, h):
            j, hs = 2 * p + xme, head_rows(h)
            return self.both(
                h,
                copy(
                    r.sp.at[j, hs],
                    r.rb.at[n2 + zme, hs],
                    self.z,
                    p * H + h,
                    dp=j,
                    got=zme * H + h,
                ),
                lambda: copy(r.tp.at[j], r.trb.at[n2 + zme], self.tz, p, dp=j, got=zme),
            )

        def from_z(self, p, h):
            j, hs = 2 * p + xme, head_rows(h)
            return self.both(
                h,
                copy(r.sp.at[j, hs], r.rb.at[n2 + p, hs], self.z, p * H + h, dp=j),
                lambda: copy(r.tp.at[j], r.trb.at[n2 + p], self.tz, p, dp=j),
            )

        def out_z(self, p, h):
            j, hs = 2 * p + xme, head_rows(h)
            s, t = self.all_s.at[me, hs], self.all_t.at[me]
            return self.both(
                h,
                copy(s, s, self.gz, p * H + h, dp=j, got=zme * H + h),
                lambda: copy(t, t, self.hz, p, dp=j, got=zme),
            )

        def in_z(self, p, h):
            j, hs = 2 * p + xme, head_rows(h)
            s, t = self.all_s.at[j, hs], self.all_t.at[j]
            return self.both(
                h,
                copy(s, s, self.gz, p * H + h, dp=j),
                lambda: copy(t, t, self.hz, p, dp=j),
            )

        def out_x(self, p, h, other=False):
            j, hs = 2 * p + (1 - xme if other else xme), head_rows(h)
            s, t = self.all_s.at[j, hs], self.all_t.at[j]
            return self.both(
                h,
                copy(s, s, self.gx, p * H + h, dp=xpart),
                lambda: copy(t, t, self.hx, p, dp=xpart),
            )

        def start(self, dup):
            for h in range(H):

                def pair(kk, h=h):
                    p = lax.rem(zme + 1 + kk, n2)
                    block = dot(r.ft[head_rows(h), :], masked_pair(everything, dup[h], p))
                    sides = block[:, :LANES].astype(BF), block[:, LANES:].astype(BF)
                    for side, values in enumerate(sides):
                        put_state(r.sp, 2 * p + side, h, values)
                    for c in self.to_x(p, h):
                        c.start()

                loop(n2, pair)

        def add_x(self, p, h):
            for c in self.to_x(p, h):
                c.wait_recv()
            j = 2 * p + xme
            if h == 0:
                r.tp[j] += r.trb[p]
            return get_state(r.sp, j, h) + get_state(r.rb, p, h)

        def near(self, h, k):
            p = lax.rem(zme + 1 + k, n2)
            put_state(r.sp, 2 * p + xme, h, self.add_x(p, h).astype(BF))
            for c in self.to_z(p, h):
                c.start()

        def own(self, h):
            r.acc[head_rows(h), :] = self.add_x(zme, h)

        def whole(self, h):
            def take(k):
                p = lax.rem(zme + 1 + k, n2)
                for c in self.from_z(p, h):
                    c.wait_recv()
                r.acc[head_rows(h), :] += get_state(r.rb, n2 + p, h)
                if h == 0:
                    r.tp[me] += r.trb[n2 + p]

            loop(n2 - 1, take)
            if h == 0:
                self.all_t[me] = r.tp[me]
            put_state(self.all_s, me, h, r.acc[head_rows(h), :].astype(BF))

            def send(k):
                for c in self.out_z(lax.rem(zme + 1 + k, n2), h):
                    c.start()

            loop(n2 - 1, send)
            for c in self.out_x(zme, h):
                c.start()

        def onward(self, h, k):
            p = lax.rem(zme + 1 + k, n2)
            for c in self.in_z(p, h):
                c.wait_recv()
            for c in self.out_x(p, h):
                c.start()

        def arrived(self, p, h):
            for c in self.out_x(p, h, other=True):
                c.wait_recv()

        def run(self, between, use, midway):
            others = n2 - 1
            if plan.big:
                for h in range(H):
                    loop(others, functools.partial(self.near, h))
                    self.own(h)
                    self.whole(h)
                between(everything=True)
                midway()
                for h in range(H):
                    loop(others, functools.partial(self.onward, h))
                for h in range(H):
                    loop(n2, lambda p, h=h: self.arrived(p, h))
            else:
                for k in range(others):
                    self.near(0, k)
                    between()
                self.own(0)
                for h in range(1, H):
                    for k in range(others):
                        if k == others - 1:
                            self.whole(h - 1)
                        self.near(h, k)
                        between()
                    self.own(h)
                between(everything=True)
                self.whole(H - 1)
                for k in range(others):
                    self.onward(0, k)
                for h in range(H):
                    for p in range(n2):
                        self.arrived(p, h)
                    if h < H - 1:
                        for k in range(others):
                            self.onward(h + 1, k)
                        use(h)
                        midway()
            for h in range(H):

                def sent(p, h=h):
                    for c in [*self.to_x(p, h), *self.out_x(p, h)]:
                        c.wait_send()

                loop(n2, sent)

                def sent_z(k, h=h):
                    p = lax.rem(zme + 1 + k, n2)
                    for c in [*self.to_z(p, h), *self.out_z(p, h)]:
                        c.wait_send()

                loop(others, sent_z)
            total = spread_totals(self.all_t[...])
            top = total.astype(BF)
            r.tot2[0 : plan.G8, :] = top
            r.tot2[plan.G8 :, :] = (total - top.astype(F32)).astype(BF)

    def put_state(ref, j, h, values):
        if plan.big:
            spot = r.stage_b.at[0, head_rows(h)]
            spot[...] = values
            pltpu.sync_copy(spot, ref.at[j, head_rows(h)])
        else:
            ref[j, head_rows(h), :] = values

    def get_state(ref, j, h):
        if plan.big:
            spot = r.stage_b.at[1, head_rows(h)]
            pltpu.sync_copy(ref.at[j, head_rows(h)], spot)
            return spot[...].astype(F32)
        return ref[j, head_rows(h), :].astype(F32)

    def state_columns(ref, p, h):
        blocks = state_pair(ref, p, r.stage_a if plan.big else None)
        return jnp.concatenate([blocks[0, head_rows(h), :], blocks[1, head_rows(h), :]], 1)

    def pick(code, product, p, rest):
        first = jnp.full((1, LANES), 1.0, F32) * (4 * p)
        rest = jnp.where(code == first, product[:, :LANES], rest)
        return jnp.where(code == first + 2.0, product[:, LANES:], rest)

    def times_state(rows, left, all_s, h):
        code, features = r.ccb[rows, :].astype(F32), left[rows, head_rows(h)]

        def pair(p, total):
            return pick(code, dot(features, state_columns(all_s, p, h)), p, total)

        total = jnp.zeros((TILE, LANES), F32)
        if plan.big:
            return lax.fori_loop(0, n2, pair, total)
        for p in range(n2):
            total = pair(p, total)
        return total

    def own_state(rows, left, all_s):
        ready = [] if plan.big else [r.num[rows, :]]
        heads = ready + [times_state(rows, left, all_s, h) for h in range(len(ready), H)]
        return halves(*(head + roll_half(head) for head in heads))

    def halves(first, second):
        return jnp.where(low, first, second)

    class Meanwhile:
        def __init__(self, each, pieces):
            self.each, self.pieces = each, list(pieces)

        def __call__(self, everything=False):
            many = len(self.pieces) if everything else self.each
            for piece in self.pieces[:many]:
                piece()
            self.pieces = self.pieces[many:]

    def early(left, all_s):
        def run(h):
            def tile(i):
                rows = rows_of(i, TILE)
                r.num[rows, :] = times_state(rows, left, all_s, h)

            loop(tiles, tile)

        return run

    first = States(
        r.sall, r.tall, ("rsx", "rtx", "rsz", "rtz", "agz", "atz", "agx", "atx")
    )
    r.tp[...] = pack_totals(dot_tn(r.oh2[:, : plan.G8], r.kf[...]))
    first.start([r.vv[0], r.vv[1]])

    onward = []

    def weights_on(which):
        for i in which:
            dst = shards[i][1]
            copy(dst.at[far], dst.at[far], "wy", i, mp=far).wait_recv()
            c = copy(dst.at[far], dst.at[far], "wc", 2 * i + 1, mp=sib)
            c.start()
            onward.append(c)

    def turn(source):
        def tile(i):
            rows = rows_of(i, TILE)
            r.ft[:, rows] = source[rows, :].astype(F32).T.astype(BF)

        return lambda: loop(tiles, tile)

    def some(body, start, count):
        return lambda: lax.fori_loop(start, start + count, lambda k, carry: (body(k), carry)[1], 0)

    quarter = tiles // 4
    first.run(
        Meanwhile(1, [some(queries, i * quarter, quarter) for i in range(4)] + [turn(r.qf)]),
        early(r.qf, r.sall),
        lambda: weights_on(range(4)),
    )

    def own_totals(rows):
        return dot(r.oh2[rows, :], r.tot2[...])

    def attend(i):
        rows = rows_of(i, TILE)
        numerator = own_state(rows, r.qf, r.sall)
        product = r.qf[rows, :].astype(F32) * own_totals(rows)
        denominator = halves(
            jnp.sum(product[:, :M], -1, keepdims=True),
            jnp.sum(product[:, M:], -1, keepdims=True),
        )
        inverse = 1.0 / denominator
        attention = numerator / denominator
        r.attf[rows, :] = attention
        r.inv[rows, :] = inverse
        r.attb[rows, :] = attention.astype(BF)

    per = plan.per
    chunk_order = [far, farsib, sib, m]
    others_mp = chunk_order[: nm - 1]

    def swap(src, dst, name, target, i):
        return copy(src, dst, name, target * per + i, mp=target, got=m * per + i)

    def swapped(dst, name, source, i):
        return copy(dst, dst, name, source * per + i, mp=source)

    def attention_copy(target, i):
        return swap(
            r.attb.at[rows_of(target * per + i, TILE)],
            r.arow.at[m, rows_of(i, TILE)],
            "a2a",
            target,
            i,
        )

    def each_tile(body, after, middle=None):
        def step(q, carry):
            i, k = q // nm, lax.rem(q, nm)
            start = lax.rem(m + (1 - k // 2) * (nm // 2), nm)
            target = start + lax.rem((k + 1) // 2, 2) * (1 - 2 * lax.rem(start, 2))
            body(target * per + i)
            pl.when(k < nm - 1)(lambda: after(target, i).start())
            return carry

        half = per // 2 * nm
        lax.fori_loop(0, half, step, 0)
        if middle is not None:
            middle()
        lax.fori_loop(half, per * nm, step, 0)

    each_tile(attend, attention_copy)
    r.arow[m] = r.attb[rows_of(m, Tm), :]

    def weights_wait(which):
        for i in which:
            dst = shards[i][1]
            own_copies[i].wait()
            copy(dst.at[sib], dst.at[sib], "wc", 2 * i, mp=sib).wait_recv()
            copy(dst.at[farsib], dst.at[farsib], "wc", 2 * i + 1, mp=sib).wait_recv()
            for c in (y_copies[i], core_copies[i], onward[i]):
                c.wait_send()

    weights_wait(range(4))
    for c in own_in:
        c.wait()

    r.small[...] = jnp.zeros((16, D), F32)

    def units(rows, s):
        up, down = r.up_g[s], r.dn_g[s]
        preact = dot(r.nm2[rows, :], up) + r.ub_g[s]
        spread = 0.5 + 0.5 * lax.erf(preact * (0.5**0.5))
        active = (preact * spread).astype(BF)
        r.act[s, rows, :] = active
        slope = spread + preact * jnp.exp(preact * preact * -0.5) * 0.3989422804014327
        grad = (dot_nt(r.cotv[rows, :], down) * slope).astype(BF)
        r.gp[s, rows, :] = grad
        r.bo[...] += dot(active, down)
        r.gn2[...] += dot_nt(grad, up)
        r.small[pl.ds(8 + s, 1), :] += jnp.sum(grad.astype(F32), 0, keepdims=True)

    gas = r.attb.reshape(nm, Tm, L)

    def grad_copy(target, i):
        rows = rows_of(i, TILE)
        return swap(gas.at[target, rows], r.gar.at[m, rows], "gaa", target, i)

    def middle_rows(i):
        rows = rows_of(i, TILE)
        for target in others_mp:
            swapped(r.arow.at[target, rows], "a2a", target, i).wait_recv()
            attention_copy(target, i).wait_send()
        columns = jnp.concatenate([r.arow[s, rows, :] for s in range(nm)], 1)
        branch = dot(columns, r.ow_g[...].reshape(D, D)).astype(BF).astype(F32)
        middle = r.tokv[rows, :].astype(F32) + branch + r.ob[...]
        hat, scale = normalised(middle)
        normed = hat * r.g2[...] + r.b2[...]
        r.mid[rows, :] = middle
        r.nm2[rows, :] = normed.astype(BF)
        r.bo[...] = jnp.zeros((TILE, D), F32)
        r.gn2[...] = jnp.zeros((TILE, D), F32)
        lax.fori_loop(0, nm, lambda s, carry: (units(rows, s), carry)[1], 0)
        middle = r.mid[rows, :]
        r.outv[rows, :] = (middle + r.bo[...] + r.db[...]).astype(BF)
        hat, scale = normalised(middle)
        upstream = r.gn2[...]
        cotangent = r.cotv[rows, :].astype(F32)
        grad = cotangent + norm_back(upstream, hat, scale, r.g2[...])
        low_grad = grad.astype(BF)
        back = dot_nt(low_grad, r.ow_g[...].reshape(D, D)).astype(BF)
        for s in range(nm):
            gas[s, rows, :] = back[:, s * L : (s + 1) * L]
        for target in others_mp:
            grad_copy(target, i).start()
        r.mid[rows, :] = grad
        r.gb[rows, :] = low_grad
        r.small[0:1, :] += jnp.sum(cotangent, 0, keepdims=True)
        r.small[1:2, :] += jnp.sum(upstream * hat, 0, keepdims=True)
        r.small[2:3, :] += jnp.sum(upstream, 0, keepdims=True)
        r.small[3:4, :] += jnp.sum(grad, 0, keepdims=True)

    lax.fori_loop(0, per, lambda i, carry: (middle_rows(i), carry)[1], 0)
    r.gar[m] = gas[m]

    up_core = [
        copy(r.upp.at[sib], r.upc.at[0], "uc", 0, mp=sib),
        copy(r.upp.at[farsib], r.upc.at[1], "uc", 1, mp=sib),
    ]
    dn_core = [
        copy(r.dnp.at[sib], r.dnc.at[0], "dc", 0, mp=sib),
        copy(r.dnp.at[farsib], r.dnc.at[1], "dc", 1, mp=sib),
    ]

    def up_part(s):
        r.upp[s] = dot_tn(r.nm2[...], r.gp[s]).astype(BF)

    def down_part(s):
        r.dnp[s, 0:hidden, :] = dot_tn(r.act[s], r.cotv[...]).astype(BF)
        r.dnp[s, hidden : hidden + L, :] = dot_tn(r.arow[s], r.gb[...]).astype(BF)

    lax.fori_loop(0, nm, lambda s, carry: (up_part(s), carry)[1], 0)
    for c in up_core:
        c.start()
    lax.fori_loop(0, nm, lambda s, carry: (down_part(s), carry)[1], 0)
    for c in dn_core:
        c.start()

    def flat_rows(ref):
        return ref.reshape(ref.shape[0] * ref.shape[1], ref.shape[2])

    def core_sum(copies, part, other, y, name):
        for c in copies:
            c.wait()
        rows = part.shape[1]

        def add(i):
            strip = rows_of(i, LANES)
            part[far, strip, :] = (
                part[far, strip, :].astype(F32) + other[1, strip, :].astype(F32)
            ).astype(BF)

        loop(rows // LANES, add)
        return copy(part.at[far], flat_rows(y).at[pl.ds(0, rows)], name, 0, mp=far)

    def y_sum(sent, part, other, y):
        sent.wait()
        flat = flat_rows(y)

        def add(i):
            strip = rows_of(i, LANES)
            flat[strip, :] = (
                part[m, strip, :].astype(F32)
                + other[0, strip, :].astype(F32)
                + flat[strip, :].astype(F32)
            ).astype(BF)

        loop(part.shape[1] // LANES, add)

    class Reduction:
        def __init__(self, source, rx, rz, out, names):
            self.source, self.rx, self.rz, self.out = source, rx, rz, out
            self.x, self.z, self.gz, self.gx = names

        def block(self, k):
            return self.source.at[xme * n2 + k]

        def to_x(self, k):
            return copy(self.source.at[(1 - xme) * n2 + k], self.rx.at[k], self.x, k, dp=xpart)

        def start(self):
            loop(n2, lambda k: self.to_x(lax.rem(zme + 1 + k, n2)).start())

        def scatter(self):
            def add(k):
                self.to_x(k).wait()
                ref = self.block(k)
                ref[...] = (ref[...].astype(F32) + self.rx[k].astype(F32)).astype(BF)

            def send(k):
                z = lax.rem(zme + 1 + k, n2)
                add(z)
                copy(self.block(z), self.rz.at[zme], self.z, z, dp=2 * z + xme, got=zme).start()

            loop(n2 - 1, send)
            add(zme)

        def gather(self):
            own = self.block(zme)

            def take(k, total):
                z = lax.rem(zme + 1 + k, n2)
                copy(self.block(z), self.rz.at[z], self.z, z, dp=2 * z + xme).wait()
                return total + self.rz[z].astype(F32)

            total = own[...].astype(F32)
            if n2 <= 4:
                for k in range(n2 - 1):
                    total = take(k, total)
            else:
                total = lax.fori_loop(0, n2 - 1, take, total)
            own[...] = total.astype(BF)
            self.place(xme * n2 + zme, 1)[...] = own[...]
            spot = self.place(xme * n2 + zme, 1)

            def send(k):
                z = lax.rem(zme + 1 + k, n2)
                copy(own, spot, self.gz, z, dp=2 * z + xme, got=zme).start()

            loop(n2 - 1, send)
            self.over_x(zme).start()

        def over_x(self, z, side=None):
            spot = self.place((xme if side is None else side) * n2 + z, 1)
            return copy(spot, spot, self.gx, z, dp=xpart)

        def spread(self):
            own = self.block(zme)

            def onward(k):
                z = lax.rem(zme + 1 + k, n2)
                copy(own, self.place(xme * n2 + z, 1), self.gz, z, dp=2 * z + xme).wait()
                self.over_x(z).start()

            loop(n2 - 1, onward)

        def finish(self):
            def wait(z):
                self.over_x(z, 1 - xme).wait_recv()
                self.over_x(z).wait_send()

            loop(n2, wait)

        def place(self, index, count):
            rows = self.source.shape[1]
            return self.out.at[pl.ds(pl.multiple_of(index * rows, rows), count * rows)]

    up = Reduction(r.upy, r.upx, r.upz, flat_rows(r.upc), ("ux", "uz", "ugz", "ugx"))
    dn = Reduction(r.dny, r.dnx, r.dnz, flat_rows(r.dnc), ("dx", "dz", "dgz", "dgx"))

    class Sums:
        def __init__(self, own, over_m, names):
            self.own, self.over_m, self.names = own, over_m, names

        def start(self):
            for target in others_mp:
                copy(
                    self.own, self.over_m.at[m], self.names[0], target, mp=target, got=m
                ).start()

        def scatter(self, send, over_d, keep):
            total = self.own[...]
            for target in others_mp:
                copy(self.own, self.over_m.at[target], self.names[0], target, mp=target).wait()
                total += self.over_m[target]
            self.send, self.over_d = send, over_d
            self.send[...] = keep(total)

            def go(k):
                j = lax.rem(me + 1 + k, n)
                copy(self.send, over_d.at[me], self.names[1], j, dp=j, got=me).start()

            loop(n - 1, go)

        def gather(self):
            self.total = self.send[...]

            def take(k, total):
                j = lax.rem(me + 1 + k, n)
                copy(self.send, self.over_d.at[j], self.names[1], j, dp=j).wait()
                return total + self.over_d[j]

            return lax.fori_loop(0, n - 1, take, self.send[...])

    small = Sums(r.small, r.small_m, ("sm", "sd"))
    last = Sums(r.last, r.last_m, ("lm", "ld"))
    small.start()
    weights_on([4])
    for i in range(per):
        for target in others_mp:
            swapped(r.gar.at[target, rows_of(i, TILE)], "gaa", target, i).wait_recv()
    up_y = core_sum(up_core, r.upp, r.upc, r.upy, "uy")
    up_y.start()

    def grad_rows(i):
        rows = rows_of(i, TILE)
        s = i // per
        inner = rows_of(i - s * per, TILE)
        grad = r.gar[s, inner, :].astype(F32)
        inv = r.inv[rows, :]
        scaled = grad * inv
        g_roll, s_roll = roll_half(grad), roll_half(scaled)
        r.gad[0, rows, :] = halves(grad, g_roll).astype(BF)
        r.gad[1, rows, :] = halves(g_roll, grad).astype(BF)
        r.gg[0, rows, :] = halves(scaled, s_roll).astype(BF)
        r.gg[1, rows, :] = halves(s_roll, scaled).astype(BF)
        product = scaled * r.attf[rows, :]
        r.gd[rows, :] = -halves(
            jnp.sum(jnp.where(low, product, 0.0), -1, keepdims=True),
            jnp.sum(jnp.where(low, 0.0, product), -1, keepdims=True),
        )

    loop(tiles, grad_rows)

    def head_column(values, h):
        return values[:, h * HD : h * HD + 1]

    head_totals = []
    for h in range(H):
        column = r.gd[:, h * HD : h * HD + 1]
        top = column.astype(BF).astype(F32)
        upper = lane((1, 2 * plan.G8)) < plan.G8
        weights = r.oh2[...] * jnp.where(upper, top, column - top).astype(BF)
        summed = dot_tn(weights, r.qf[:, h * M : (h + 1) * M])
        head_totals.append(summed[: plan.G8] + summed[plan.G8 :])
    r.tp[...] = pack_totals(jnp.concatenate(head_totals, 1))
    dn_y = core_sum(dn_core, r.dnp, r.dnc, r.dny, "dy")
    dn_y.start()
    second = States(
        r.gall, r.gtall, ("gsx", "gtx", "gsz", "gtz", "ggz", "hgz", "ggx", "hgx")
    )
    second.start([r.gg[0], r.gg[1]])

    def contract(rows, dup, all_s, h):
        def pair(p, total):
            return total + dot_nt(masked_pair(rows, dup[h, rows, :], p), state_columns(all_s, p, h))

        total = jnp.zeros((TILE, M), F32)
        if plan.big:
            return lax.fori_loop(0, n2, pair, total)
        for p in range(n2):
            total = pair(p, total)
        return total

    def early_keys(h):
        def tile(i):
            rows = rows_of(i, TILE)
            r.gkf[rows, :] = contract(rows, r.vv, r.gall, h)

        loop(tiles, tile)
        early(r.kf, r.gall)(h)

    def feature_back(rows, which, grad_features):
        u = r.qk[which, rows, :]
        weighted = (grad_features * phi(u)).astype(BF)
        both = dot(weighted, r.wb[...])
        return (
            both[:, :L] * SCALE - both[:, L:] * u.astype(F32) * (SCALE * SCALE)
        ).astype(BF)

    def query_back(i):
        rows = rows_of(i, TILE)
        totals = own_totals(rows)
        inv, gd = r.inv[rows, :], r.gd[rows, :]
        parts = [
            contract(rows, r.gad, r.sall, h) * head_column(inv, h)
            + totals[:, h * M : (h + 1) * M] * head_column(gd, h)
            for h in range(H)
        ]
        r.grads[0, rows, :] = feature_back(rows, 0, jnp.concatenate(parts, 1))

    def own_unit_sums(total):
        rows = lax.broadcasted_iota(jnp.int32, (16, 1), 0)
        units_row = jnp.sum(jnp.where(rows == 8 + m, total, 0.0), 0, keepdims=True)
        return jnp.concatenate([total[0:4], units_row, jnp.zeros((3, D), F32)], 0)

    def small_scatter():
        small.scatter(r.small_s, r.small_d, own_unit_sums)

    def send_query_grads():
        for target in others_mp:
            copy(
                r.grads.at[0, rows_of(target, Tm)], r.garr.at[m, 0], "grq", target, mp=target, got=m
            ).start()

    def query_projection():
        part = dot(r.ft[...], r.grads[0]).astype(BF)
        flat = flat_rows(r.dny)
        for c in range(D // L):
            flat[plan.rest : plan.tail, c * L : (c + 1) * L] = part[c * L : (c + 1) * L, :]

    gtv = r.nm2
    out_land, tok_land = flat_rows(r.dn_g), flat_rows(r.up_g)
    out_y = copy(r.outv, out_land.at[mine], "oy", 0, mp=far)
    out_core = copy(r.outv, out_land.at[mine], "oc", 0, mp=sib)

    def start_up():
        y_sum(up_y, r.upp, r.upc, r.upy)
        up.start()

    def midway():
        y_sum(dn_y, r.dnp, r.dnc, r.dny)
        dn.start()
        out_y.start()
        out_core.start()
        up.scatter()

    def together(*bodies):
        def run():
            for body in bodies:
                body()

        return run

    second.run(
        Meanwhile(
            1,
            [
                some(query_back, 0, quarter),
                some(query_back, quarter, quarter),
                some(query_back, 2 * quarter, quarter),
                together(some(query_back, 3 * quarter, quarter), send_query_grads),
                turn(r.nm),
                together(query_projection, start_up, small_scatter),
            ],
        ),
        early_keys,
        midway,
    )
    dn.scatter()
    out_land[mine, :] = r.outv[...]
    def key_back(i):
        rows = rows_of(i, TILE)
        totals = own_totals(rows)
        ready = [] if plan.big else [r.gkf[rows, :]]
        parts = ready + [contract(rows, r.vv, r.gall, h) for h in range(len(ready), H)]
        gkf = jnp.concatenate(parts, 1)
        r.grads[1, rows, :] = feature_back(rows, 1, gkf + totals)
        r.grads[2, rows, :] = own_state(rows, r.kf, r.gall).astype(BF)

    both = pl.ds(1, 2)

    def key_copy(target, i):
        return swap(
            r.grads.at[both, rows_of(target * per + i, TILE)],
            r.garr.at[m, both, rows_of(i, TILE)],
            "grk",
            target,
            i,
        )

    each_tile(key_back, key_copy, up.gather)
    for a in range(3):
        r.garr[m, a] = r.grads[a, rows_of(m, Tm), :]

    part = dot(r.ft[...], jnp.concatenate([r.grads[1], r.grads[2]], 1)).astype(BF)
    flat = flat_rows(r.kvp)
    flat[0:D, :] = part[:, :L]
    flat[D : 2 * D, :] = part[:, L:]

    def kv_send(k):
        j = lax.rem(me + 1 + k, n)
        copy(r.kvp.at[j], r.kvr.at[me], "ks", j, dp=j, got=me).start()

    loop(n - 1, kv_send)

    out_far = out_land.at[rows_of(far, Tm)]
    copy(out_far, out_far, "oy", 0, mp=far).wait_recv()
    out_on = copy(out_far, out_far, "oc", 1, mp=sib)
    out_on.start()

    for target in others_mp:
        copy(r.garr.at[target, 0], r.garr.at[target, 0], "grq", target, mp=target).wait_recv()
    weights_wait([4])
    r.ends[...] = jnp.zeros((8, D), F32)
    tok_sent = []

    quarters = D // LANES

    def send_ends():
        for row in range(2):
            for q in range(quarters):
                spot = row * quarters + q
                r.last[spot : spot + 1, :] = r.ends[row : row + 1, q * LANES : (q + 1) * LANES]
        last.start()

    def norm1_back(i):
        rows = rows_of(i, TILE)
        for target in others_mp:
            swapped(r.garr.at[target, both, rows], "grk", target, i).wait_recv()
        upstream = jnp.zeros((TILE, D), F32)
        for s in range(nm):
            left = jnp.concatenate([r.garr[s, a, rows, :] for a in range(3)], 1)
            right = jnp.concatenate([r.wq_g[s, a] for a in range(3)], 1)
            upstream += dot_nt(left, right)
        upstream = upstream.astype(BF).astype(F32)
        hat, scale = normalised(r.tokv[rows, :].astype(F32))
        gtv[rows, :] = (r.mid[rows, :] + norm_back(upstream, hat, scale, r.g1[...])).astype(BF)
        r.ends[0:1, :] += jnp.sum(upstream * hat, 0, keepdims=True)
        r.ends[1:2, :] += jnp.sum(upstream, 0, keepdims=True)
        if i == per - 1:
            send_ends()
        spot = tok_land.at[rows_of(m * per + i, TILE)]
        copies = [
            copy(gtv.at[rows], spot, "ty", i, mp=far),
            copy(gtv.at[rows], spot, "tc", 2 * i, mp=sib),
        ]
        for c in copies:
            c.start()
        tok_sent.append(copies)

    for i in range(per):
        norm1_back(i)
        if i == 0:
            dn.gather()
            up.spread()
    tok_land[mine, :] = gtv[...]

    def kv_sum():
        total = r.kvp[me].astype(F32)

        def take(k, total):
            j = lax.rem(me + 1 + k, n)
            copy(r.kvp.at[j], r.kvr.at[j], "ks", j, dp=j).wait()
            return total + r.kvr[j].astype(F32)

        r.kvp[me] = lax.fori_loop(0, n - 1, take, total).astype(BF)

    kv_sum()
    last.scatter(r.last, r.last_d, lambda total: total)
    kv_spot = r.kvl.at[me]
    r.kvl[me] = r.kvp[me]

    def kv_spread(k):
        j = lax.rem(me + 1 + k, n)
        copy(r.kvp.at[me], kv_spot, "kg", j, dp=j, got=me).start()

    loop(n - 1, kv_spread)
    dn.spread()
    tok_on = []

    def tok_forward(i):
        spot = tok_land.at[rows_of(far * per + i, TILE)]
        copy(spot, spot, "ty", i, mp=far).wait_recv()
        c = copy(spot, spot, "tc", 2 * i + 1, mp=sib)
        c.start()
        tok_on.append(c)

    sums = small.gather()
    ends = last.gather()
    r.small_o[0:4, :] = sums[0:4]
    for row in range(2):
        for q in range(quarters):
            spot = row * quarters + q
            r.small_o[4 + row : 5 + row, q * LANES : (q + 1) * LANES] = ends[spot : spot + 1]
    r.small_o[6:7, :] = sums[4:5]

    written = []

    def write(src, dst):
        c = local(src, dst, len(written))
        c.start()
        written.append(c)

    def kv_wait(k):
        j = lax.rem(me + 1 + k, n)
        copy(r.kvp.at[me], r.kvl.at[j], "kg", j, dp=j).wait()

    for index, owner in enumerate((sib, farsib)):
        spot = out_land.at[rows_of(owner, Tm)]
        copy(spot, spot, "oc", index, mp=sib).wait_recv()
    write(out_land, r.out_o)
    for i in range(per):
        tok_forward(i)
    up.finish()
    write(up.out.at[pl.ds(0, D)], r.upg_o)
    loop(n - 1, kv_wait)
    write(flat_rows(r.kvl).at[pl.ds(0, 2 * D)], r.kvg_o)
    for i in range(per):
        for index, owner in enumerate((sib, farsib)):
            spot = tok_land.at[rows_of(owner * per + i, TILE)]
            copy(spot, spot, "tc", 2 * i + index, mp=sib).wait_recv()
    write(tok_land, r.gtok_o)
    dn.finish()
    write(dn.out.at[pl.ds(0, plan.tail)], r.dng_o)
    for y, core in tok_sent:
        y.wait_send()
        core.wait_send()
    for c in (out_y, out_core, out_on, *tok_on):
        c.wait_send()
    for c in written:
        c.wait()
    for target in others_mp:
        for i in range(per):
            for c in (grad_copy(target, i), key_copy(target, i)):
                c.wait_send()
        copy(r.grads.at[0, rows_of(target, Tm)], r.garr.at[m, 0], "grq", target, mp=target).wait_send()


def widen_kernel(plan, *refs):
    (output, tokens, up, down, kv, small), refs = refs[:6], refs[6:]
    (out_o, tok_o, qkv_o, ow_o, ob_o, g1_o, b1_o, g2_o, b2_o, up_o, ub_o, dn_o, db_o), refs = (
        refs[:13],
        refs[13:],
    )
    tok_v, out_v, up_v, dn_v, kv_v, tok_w, up_w, dn_w, ow_w, qkv_w, sem_in, sem_out = refs
    D, L, hidden, T = plan.D, plan.L, plan.F, plan.T
    pieces = 4
    size = T // pieces
    reads = [
        pltpu.make_async_copy(a, b, sem_in.at[i])
        for i, (a, b) in enumerate([(up, up_v), (down, dn_v), (kv, kv_v), (output, out_v)])
    ]
    token_reads = [
        pltpu.make_async_copy(
            tokens.at[pl.ds(i * size, size)], tok_v.at[pl.ds(i * size, size)], sem_in.at[4 + i]
        )
        for i in range(pieces)
    ]
    for c in token_reads + reads:
        c.start()
    for row, ref in ((3, ob_o), (4, g1_o), (5, b1_o), (1, g2_o), (2, b2_o), (6, ub_o), (0, db_o)):
        ref[...] = small[row : row + 1, :]
    writes = []

    def send(src, dst):
        c = pltpu.make_async_copy(src, dst, sem_out.at[len(writes)])
        c.start()
        writes.append(c)

    for i in range(pieces):
        token_reads[i].wait()
        rows = pl.ds(i * size, size)
        tok_w[rows, :] = tok_v[rows, :].astype(F32)
        send(tok_w.at[rows], tok_o.at[rows])
    for c in reads:
        c.wait()
    send(out_v, out_o)
    up_w[...] = up_v[...].astype(F32)
    send(up_w, up_o)
    dn_w[...] = dn_v[0:hidden, :].astype(F32)
    send(dn_w, dn_o)
    ow_w[...] = dn_v[hidden : hidden + L, :].astype(F32)
    send(ow_w, ow_o)
    for c in range(D // L):
        qkv_w[0, c * L : (c + 1) * L, :] = dn_v[
            plan.rest : plan.tail, c * L : (c + 1) * L
        ].astype(F32)
    qkv_w[1] = kv_v[0:D, :].astype(F32)
    qkv_w[2] = kv_v[D : 2 * D, :].astype(F32)
    send(qkv_w, qkv_o)
    for c in writes:
        c.wait()


def widen(plan, *gathered):
    D, L, hidden, T = plan.D, plan.L, plan.F, plan.T
    line = ("vmem", (1, D))
    outs = [
        ("hbm", (T, D)),
        ("hbm", (T, D)),
        ("hbm", (3, D, L)),
        ("hbm", (L, D)),
        *[line] * 5,
        ("hbm", (D, hidden)),
        ("vmem", (1, hidden)),
        ("hbm", (hidden, D)),
        line,
    ]
    spaces = {"vmem": pltpu.VMEM, "hbm": pl.ANY}
    results = pl.pallas_call(
        functools.partial(widen_kernel, plan),
        out_shape=[
            jax.ShapeDtypeStruct(shape, BF if i == 0 else F32) for i, (_, shape) in enumerate(outs)
        ],
        in_specs=[pl.BlockSpec(memory_space=pl.ANY)] * 5 + [pl.BlockSpec(memory_space=pltpu.VMEM)],
        out_specs=[pl.BlockSpec(memory_space=spaces[kind]) for kind, _ in outs],
        scratch_shapes=[
            pltpu.VMEM((T, D), BF),
            pltpu.VMEM((T, D), BF),
            pltpu.VMEM((D, hidden), BF),
            pltpu.VMEM((plan.tail, D), BF),
            pltpu.VMEM((2 * D, L), BF),
            pltpu.VMEM((T, D), F32),
            pltpu.VMEM((D, hidden), F32),
            pltpu.VMEM((hidden, D), F32),
            pltpu.VMEM((L, D), F32),
            pltpu.VMEM((3, D, L), F32),
            pltpu.SemaphoreType.DMA((8,)),
            pltpu.SemaphoreType.DMA((16,)),
        ],
        compiler_params=pltpu.CompilerParams(vmem_limit_bytes=60 << 20),
        name="widen",
    )(*gathered)
    return tuple(v.reshape(-1) if v.shape[0] == 1 else v for v in results)


def per_device(
    n,
    nm,
    tokens,
    cotangent,
    bucket,
    cell,
    features,
    qkv_weight,
    out_weight,
    out_bias,
    norm1_gain,
    norm1_bias,
    norm2_gain,
    norm2_bias,
    up_weight,
    up_bias,
    down_weight,
    down_bias,
):
    count, width = tokens.shape
    local, hidden = qkv_weight.shape[2], up_weight.shape[1]
    plan = Plan(n, nm, count, width, local, features.shape[2], hidden)
    spaces = {"vmem": pltpu.VMEM, "hbm": pl.ANY}
    line = lambda v: v.reshape(1, -1)
    grid_ids = (count // LANES, LANES)
    outs = pl.pallas_call(
        functools.partial(layer_kernel, plan),
        out_shape=[jax.ShapeDtypeStruct(s, d) for _, _, s, d in plan.outputs],
        in_specs=[pl.BlockSpec(memory_space=spaces[k]) for _, k in plan.inputs],
        out_specs=[pl.BlockSpec(memory_space=spaces[k]) for _, k, _, _ in plan.outputs],
        scratch_shapes=[pltpu.VMEM(s, d) for _, s, d in plan.scratch]
        + [pltpu.SemaphoreType.DMA((c,)) for c in plan.sems.values() for _ in range(2)]
        + [pltpu.SemaphoreType.DMA((plan.local_sems,))],
        compiler_params=pltpu.CompilerParams(
            collective_id=1, has_side_effects=True, vmem_limit_bytes=63 << 20
        ),
        name="performer_layer",
    )(
        tokens,
        bucket.reshape(grid_ids),
        cell.reshape(grid_ids),
        features,
        qkv_weight,
        line(norm1_gain),
        line(norm1_bias),
        line(out_bias),
        line(norm2_gain),
        line(norm2_bias),
        line(down_bias),
        cotangent,
        out_weight,
        up_weight,
        line(up_bias),
        down_weight,
    )
    return widen(plan, *outs[:6])


def solution(mesh):
    return jax.shard_map(
        functools.partial(per_device, mesh.shape["dp"], mesh.shape["mp"]),
        mesh=mesh,
        in_specs=(
            P("dp", None),
            P("dp", None),
            P("dp", None),
            P("dp"),
            P(),
            P(None, None, "mp"),
            P("mp", None),
            P(),
            P(),
            P(),
            P(),
            P(),
            P(None, "mp"),
            P("mp"),
            P("mp", None),
            P(),
        ),
        out_specs=(
            P("dp", None),
            P("dp", None),
            P(None, None, "mp"),
            P("mp", None),
            P(),
            P(),
            P(),
            P(),
            P(),
            P(None, "mp"),
            P("mp"),
            P("mp", None),
            P(),
        ),
        check_vma=False,
    )
```

profile of v0, /device:TPU:12, one launch (start us, length us, event | category | flops | bytes accessed | tf_op | source)
XLA Modules:
  0.0 165.7 jit_solution(16942162850965612409)
XLA Ops:
  0.7 156.8 %performer_layer.1 = (bf16[2048,512]{1,0:T(8,128)(2,1)}, bf16[2048,512]{1,0:T(8,128)(2,1)}, bf16[512,512]{1,0:T(8,128)(2,1)}, bf16[768,512]{1,0:T(8,128)(2,1)}, ...) custom-call(bf16[2048,512]{1,0:T(8,128)(2,1)} %refs_0_.1, s32[16,128]{1,0:T(8,128)} %bitcast.16, s32[16,128]{1,0:T(8,128)} %bitcast.17, ...), custom_call_target="tpu_custom_call" | custom-call | tf_op jit(solution)/shard_map/performer_layer/pallas_call | solution.py:1440
  157.4 8.1 %widen.1 = (bf16[2048,512]{1,0:T(8,128)(2,1)}, f32[2048,512]{1,0:T(8,128)}, f32[3,512,128]{2,1,0:T(8,128)}, f32[128,512]{1,0:T(8,128)}, f32[1,512]{1,0:T(1,128)}...) custom-call(bf16[2048,512]{1,0:T(8,128)(2,1)} %get-tuple-element.32., ...), custom_call_target="tpu_custom_call" | custom-call | tf_op jit(solution)/shard_map/widen/pallas_call | solution.py:1387
where the time goes:
time: 168 us; the launch traced here: 166 us
  Pallas kernels  165 us (98%)
    pallas_call x1, Pallas kernels, per_device(): pl.pallas_call(functools.partial(layer_kernel, plan), out_shape=[jax.Shap...  157 us
    pallas_call x1, Pallas kernels, widen(): pl.pallas_call(functools.partial(widen_kernel, plan), out_shape=[jax.Shap...  8.06 us

commit v1 on v0

--- a/solution.py
+++ b/solution.py
@@ -240,7 +240,7 @@
             "lm": nm,
             "ld": n,
         }
-        self.local_sems = 16
+        self.local_sems = 24
 
     def names(self):
         return (
@@ -268,6 +268,7 @@
     hidden = plan.F
     n2 = n // 2
     tiles = T // TILE
+    wide = TILE if plan.big else 2 * TILE
     me, m = lax.axis_index("dp"), lax.axis_index("mp")
     sib = m + 1 - 2 * lax.rem(m, 2)
     far = lax.rem(m + nm // 2, nm)
@@ -309,9 +310,14 @@
         )
 
     mine = rows_of(m, Tm)
-    tok_in = local(r.tok, r.nm, 10)
-    own_in = [local(r.cot.at[mine], r.cotv, 0), local(r.tok.at[mine], r.tokv, 11)]
-    for c in [tok_in, *own_in]:
+    wides, len_shards = T // wide, 5
+
+    def tok_in(i):
+        rows = rows_of(i, wide)
+        return local(r.tok.at[rows], r.nm.at[rows], 1 + len_shards + i)
+
+    own_in = [local(r.cot.at[mine], r.cotv, 0), local(r.tok.at[mine], r.tokv, 1 + len_shards + wides)]
+    for c in [tok_in(i) for i in range(wides)] + own_in:
         c.start()
 
     r.wcat[:, 0:L] = r.wqkv[0]
@@ -364,11 +370,11 @@
         shift = jnp.where(lane((1, HM)) < M, first, second) * HALF_SQUARE
         return jnp.exp(projected - shift)
 
-    tok_in.wait()
     pl.semaphore_wait(barrier, n - 1 + nm - 1)
 
     def project(i):
-        rows = rows_of(i, TILE)
+        rows = rows_of(i, wide)
+        tok_in(i).wait()
         hat, _ = normalised(r.nm[rows, :].astype(F32))
         normed = (hat * r.g1[...] + r.b1[...]).astype(BF)
         r.nm[rows, :] = normed
@@ -376,12 +382,12 @@
         k = u[:, 0:L]
         r.qk[1, rows, :] = k
         r.vv[0, rows, :], r.vv[1, rows, :] = u[:, L : 2 * L], u[:, 2 * L : 3 * L]
-        features = phi(k)
-        r.kf[rows, :] = features.astype(BF)
-        r.ft[:, rows] = features.T.astype(BF)
+        features = phi(k).astype(BF)
+        r.kf[rows, :] = features
+        r.ft[:, rows] = features.T
 
     def queries(i):
-        rows = rows_of(i, TILE)
+        rows = rows_of(i, wide)
         q = dot(r.nm[rows, :], r.wcat[:, 0:L]).astype(BF)
         r.qk[0, rows, :] = q
         r.qf[rows, :] = phi(q).astype(BF)
@@ -400,7 +406,7 @@
         core_copies.append(copy(src, dst.at[m], "wc", 2 * i, mp=sib))
     for c in own_copies + y_copies + core_copies:
         c.start()
-    loop(tiles, project)
+    lax.fori_loop(0, wides, lambda i, carry: (project(i), carry)[1], 0)
 
     def state_pair(ref, p, stage):
         if plan.big:
@@ -418,7 +424,30 @@
     everything = pl.ds(0, T)
 
     def head_rows(h):
-        return pl.ds(h * M, M)
+        return pl.ds(h * M, M) if isinstance(h, int) else pl.ds(pl.multiple_of(h * M, M), M)
+
+    def at_first(h, body):
+        if isinstance(h, int):
+            if h == 0:
+                body()
+        else:
+            pl.when(h == 0)(body)
+
+    class Pair:
+        def __init__(self, h, state, totals):
+            self.h, self.state, self.totals = h, state, totals
+
+        def start(self):
+            self.state.start()
+            at_first(self.h, lambda: self.totals().start())
+
+        def wait_recv(self):
+            self.state.wait_recv()
+            at_first(self.h, lambda: self.totals().wait_recv())
+
+        def wait_send(self):
+            self.state.wait_send()
+            at_first(self.h, lambda: self.totals().wait_send())
 
     class States:
         def __init__(self, all_s, all_t, names):
@@ -426,7 +455,7 @@
             self.x, self.tx, self.z, self.tz, self.gz, self.hz, self.gx, self.hx = names
 
         def both(self, h, state, totals):
-            return [state, totals()] if h == 0 else [state]
+            return Pair(h, state, totals)
 
         def to_x(self, p, h):
             j, hs = 2 * p + 1 - xme, head_rows(h)
@@ -487,32 +516,30 @@
             )
 
         def start(self, dup):
-            for h in range(H):
-
-                def pair(kk, h=h):
-                    p = lax.rem(zme + 1 + kk, n2)
-                    block = dot(r.ft[head_rows(h), :], masked_pair(everything, dup[h], p))
-                    sides = block[:, :LANES].astype(BF), block[:, LANES:].astype(BF)
-                    for side, values in enumerate(sides):
-                        put_state(r.sp, 2 * p + side, h, values)
-                    for c in self.to_x(p, h):
-                        c.start()
-
-                loop(n2, pair)
+            def pair(q, carry):
+                h, p = q // n2, lax.rem(zme + 1 + lax.rem(q, n2), n2)
+                block = dot(r.ft[head_rows(h), :], masked_pair(everything, dup[h], p))
+                put_state(r.sp, 2 * p, h, block[:, :LANES].astype(BF))
+                put_state(r.sp, 2 * p + 1, h, block[:, LANES:].astype(BF))
+                self.to_x(p, h).start()
+                return carry
+
+            lax.fori_loop(0, H * n2, pair, 0)
 
         def add_x(self, p, h):
-            for c in self.to_x(p, h):
-                c.wait_recv()
+            self.to_x(p, h).wait_recv()
             j = 2 * p + xme
-            if h == 0:
+
+            def totals():
                 r.tp[j] += r.trb[p]
+
+            at_first(h, totals)
             return get_state(r.sp, j, h) + get_state(r.rb, p, h)
 
         def near(self, h, k):
             p = lax.rem(zme + 1 + k, n2)
             put_state(r.sp, 2 * p + xme, h, self.add_x(p, h).astype(BF))
-            for c in self.to_z(p, h):
-                c.start()
+            self.to_z(p, h).start()
 
         def own(self, h):
             r.acc[head_rows(h), :] = self.add_x(zme, h)
@@ -520,8 +547,7 @@
         def whole(self, h):
             def take(k):
                 p = lax.rem(zme + 1 + k, n2)
-                for c in self.from_z(p, h):
-                    c.wait_recv()
+                self.from_z(p, h).wait_recv()
                 r.acc[head_rows(h), :] += get_state(r.rb, n2 + p, h)
                 if h == 0:
                     r.tp[me] += r.trb[n2 + p]
@@ -532,73 +558,53 @@
             put_state(self.all_s, me, h, r.acc[head_rows(h), :].astype(BF))
 
             def send(k):
-                for c in self.out_z(lax.rem(zme + 1 + k, n2), h):
-                    c.start()
+                self.out_z(lax.rem(zme + 1 + k, n2), h).start()
 
             loop(n2 - 1, send)
-            for c in self.out_x(zme, h):
-                c.start()
+            self.out_x(zme, h).start()
 
         def onward(self, h, k):
             p = lax.rem(zme + 1 + k, n2)
-            for c in self.in_z(p, h):
-                c.wait_recv()
-            for c in self.out_x(p, h):
-                c.start()
+            self.in_z(p, h).wait_recv()
+            self.out_x(p, h).start()
 
         def arrived(self, p, h):
-            for c in self.out_x(p, h, other=True):
-                c.wait_recv()
-
-        def run(self, between, use, midway):
+            self.out_x(p, h, other=True).wait_recv()
+
+        def run(self, work, rest, use, midway):
             others = n2 - 1
-            if plan.big:
-                for h in range(H):
-                    loop(others, functools.partial(self.near, h))
-                    self.own(h)
-                    self.whole(h)
-                between(everything=True)
-                midway()
-                for h in range(H):
-                    loop(others, functools.partial(self.onward, h))
-                for h in range(H):
-                    loop(n2, lambda p, h=h: self.arrived(p, h))
-            else:
-                for k in range(others):
-                    self.near(0, k)
-                    between()
-                self.own(0)
-                for h in range(1, H):
-                    for k in range(others):
-                        if k == others - 1:
-                            self.whole(h - 1)
-                        self.near(h, k)
-                        between()
-                    self.own(h)
-                between(everything=True)
-                self.whole(H - 1)
-                for k in range(others):
-                    self.onward(0, k)
-                for h in range(H):
-                    for p in range(n2):
-                        self.arrived(p, h)
-                    if h < H - 1:
-                        for k in range(others):
-                            self.onward(h + 1, k)
-                        use(h)
-                        midway()
+            steps = H * others
+
+            def step(q, carry):
+                h, k = q // others, lax.rem(q, others)
+                pl.when(q == steps - 1)(lambda: self.whole(0))
+                self.near(h, k)
+                work(q)
+                pl.when(k == others - 1)(lambda: self.own(h))
+                return carry
+
+            lax.fori_loop(0, steps, step, 0)
+            rest()
+            self.whole(H - 1)
+            loop(others, lambda k: self.onward(0, k))
             for h in range(H):
+                loop(n2, lambda p, h=h: self.arrived(p, h))
+                if h < H - 1:
+                    loop(others, lambda k, h=h: self.onward(h + 1, k))
+                    use(h)
+                    midway()
+            for h in range(H):
 
                 def sent(p, h=h):
-                    for c in [*self.to_x(p, h), *self.out_x(p, h)]:
-                        c.wait_send()
+                    self.to_x(p, h).wait_send()
+                    self.out_x(p, h).wait_send()
 
                 loop(n2, sent)
 
                 def sent_z(k, h=h):
                     p = lax.rem(zme + 1 + k, n2)
-                    for c in [*self.to_z(p, h), *self.out_z(p, h)]:
-                        c.wait_send()
+                    self.to_z(p, h).wait_send()
+                    self.out_z(p, h).wait_send()
 
                 loop(others, sent_z)
             total = spread_totals(self.all_t[...])
@@ -636,7 +642,7 @@
         def pair(p, total):
             return pick(code, dot(features, state_columns(all_s, p, h)), p, total)
 
-        total = jnp.zeros((TILE, LANES), F32)
+        total = jnp.zeros((rows.size, LANES), F32)
         if plan.big:
             return lax.fori_loop(0, n2, pair, total)
         for p in range(n2):
@@ -651,23 +657,17 @@
     def halves(first, second):
         return jnp.where(low, first, second)
 
-    class Meanwhile:
-        def __init__(self, each, pieces):
-            self.each, self.pieces = each, list(pieces)
-
-        def __call__(self, everything=False):
-            many = len(self.pieces) if everything else self.each
-            for piece in self.pieces[:many]:
-                piece()
-            self.pieces = self.pieces[many:]
-
     def early(left, all_s):
         def run(h):
-            def tile(i):
-                rows = rows_of(i, TILE)
+            if plan.big:
+                return
+
+            def tile(i, carry):
+                rows = rows_of(i, wide)
                 r.num[rows, :] = times_state(rows, left, all_s, h)
-
-            loop(tiles, tile)
+                return carry
+
+            lax.fori_loop(0, wides, tile, 0)
 
         return run
 
@@ -675,7 +675,7 @@
         r.sall, r.tall, ("rsx", "rtx", "rsz", "rtz", "agz", "atz", "agx", "atx")
     )
     r.tp[...] = pack_totals(dot_tn(r.oh2[:, : plan.G8], r.kf[...]))
-    first.start([r.vv[0], r.vv[1]])
+    first.start(r.vv)
 
     onward = []
 
@@ -690,16 +690,25 @@
     def turn(source):
         def tile(i):
             rows = rows_of(i, TILE)
-            r.ft[:, rows] = source[rows, :].astype(F32).T.astype(BF)
+            r.ft[:, rows] = source[rows, :].T
 
         return lambda: loop(tiles, tile)
 
-    def some(body, start, count):
-        return lambda: lax.fori_loop(start, start + count, lambda k, carry: (body(k), carry)[1], 0)
-
-    quarter = tiles // 4
+    def in_quarters(body, size):
+        quarter = T // size // 4
+
+        def work(q):
+            def tile(i, carry):
+                body(q * quarter + i)
+                return carry
+
+            pl.when(q < 4)(lambda: (lax.fori_loop(0, quarter, tile, 0), None)[1])
+
+        return work
+
     first.run(
-        Meanwhile(1, [some(queries, i * quarter, quarter) for i in range(4)] + [turn(r.qf)]),
+        in_quarters(queries, wide),
+        turn(r.qf),
         early(r.qf, r.sall),
         lambda: weights_on(range(4)),
     )
@@ -1009,9 +1018,9 @@
     up_y.start()
 
     def grad_rows(i):
-        rows = rows_of(i, TILE)
-        s = i // per
-        inner = rows_of(i - s * per, TILE)
+        rows = rows_of(i, wide)
+        s = i // (Tm // wide)
+        inner = rows_of(i - s * (Tm // wide), wide)
         grad = r.gar[s, inner, :].astype(F32)
         inv = r.inv[rows, :]
         scaled = grad * inv
@@ -1026,7 +1035,7 @@
             jnp.sum(jnp.where(low, 0.0, product), -1, keepdims=True),
         )
 
-    loop(tiles, grad_rows)
+    lax.fori_loop(0, wides, lambda i, carry: (grad_rows(i), carry)[1], 0)
 
     def head_column(values, h):
         return values[:, h * HD : h * HD + 1]
@@ -1045,13 +1054,13 @@
     second = States(
         r.gall, r.gtall, ("gsx", "gtx", "gsz", "gtz", "ggz", "hgz", "ggx", "hgx")
     )
-    second.start([r.gg[0], r.gg[1]])
+    second.start(r.gg)
 
     def contract(rows, dup, all_s, h):
         def pair(p, total):
             return total + dot_nt(masked_pair(rows, dup[h, rows, :], p), state_columns(all_s, p, h))
 
-        total = jnp.zeros((TILE, M), F32)
+        total = jnp.zeros((rows.size, M), F32)
         if plan.big:
             return lax.fori_loop(0, n2, pair, total)
         for p in range(n2):
@@ -1059,11 +1068,15 @@
         return total
 
     def early_keys(h):
-        def tile(i):
-            rows = rows_of(i, TILE)
+        if plan.big:
+            return
+
+        def tile(i, carry):
+            rows = rows_of(i, wide)
             r.gkf[rows, :] = contract(rows, r.vv, r.gall, h)
-
-        loop(tiles, tile)
+            return carry
+
+        lax.fori_loop(0, wides, tile, 0)
         early(r.kf, r.gall)(h)
 
     def feature_back(rows, which, grad_features):
@@ -1075,7 +1088,7 @@
         ).astype(BF)
 
     def query_back(i):
-        rows = rows_of(i, TILE)
+        rows = rows_of(i, wide)
         totals = own_totals(rows)
         inv, gd = r.inv[rows, :], r.gd[rows, :]
         parts = [
@@ -1121,30 +1134,17 @@
         out_core.start()
         up.scatter()
 
-    def together(*bodies):
-        def run():
-            for body in bodies:
-                body()
-
-        return run
-
-    second.run(
-        Meanwhile(
-            1,
-            [
-                some(query_back, 0, quarter),
-                some(query_back, quarter, quarter),
-                some(query_back, 2 * quarter, quarter),
-                together(some(query_back, 3 * quarter, quarter), send_query_grads),
-                turn(r.nm),
-                together(query_projection, start_up, small_scatter),
-            ],
-        ),
-        early_keys,
-        midway,
-    )
+    def after_queries():
+        send_query_grads()
+        turn(r.nm)()
+        query_projection()
+        start_up()
+        small_scatter()
+
+    second.run(in_quarters(query_back, wide), after_queries, early_keys, midway)
     dn.scatter()
     out_land[mine, :] = r.outv[...]
+
     def key_back(i):
         rows = rows_of(i, TILE)
         totals = own_totals(rows)
@@ -1189,7 +1189,6 @@
         copy(r.garr.at[target, 0], r.garr.at[target, 0], "grq", target, mp=target).wait_recv()
     weights_wait([4])
     r.ends[...] = jnp.zeros((8, D), F32)
-    tok_sent = []
 
     quarters = D // LANES
 
@@ -1214,22 +1213,24 @@
         gtv[rows, :] = (r.mid[rows, :] + norm_back(upstream, hat, scale, r.g1[...])).astype(BF)
         r.ends[0:1, :] += jnp.sum(upstream * hat, 0, keepdims=True)
         r.ends[1:2, :] += jnp.sum(upstream, 0, keepdims=True)
-        if i == per - 1:
-            send_ends()
+        pl.when(i == per - 1)(send_ends)
+        for c in tok_copies(i):
+            c.start()
+
+        @pl.when(i == 0)
+        def _():
+            dn.gather()
+            up.spread()
+
+    def tok_copies(i):
+        rows = rows_of(i, TILE)
         spot = tok_land.at[rows_of(m * per + i, TILE)]
-        copies = [
+        return (
             copy(gtv.at[rows], spot, "ty", i, mp=far),
             copy(gtv.at[rows], spot, "tc", 2 * i, mp=sib),
-        ]
-        for c in copies:
-            c.start()
-        tok_sent.append(copies)
-
-    for i in range(per):
-        norm1_back(i)
-        if i == 0:
-            dn.gather()
-            up.spread()
+        )
+
+    lax.fori_loop(0, per, lambda i, carry: (norm1_back(i), carry)[1], 0)
     tok_land[mine, :] = gtv[...]
 
     def kv_sum():
@@ -1299,9 +1300,9 @@
     write(tok_land, r.gtok_o)
     dn.finish()
     write(dn.out.at[pl.ds(0, plan.tail)], r.dng_o)
-    for y, core in tok_sent:
-        y.wait_send()
-        core.wait_send()
+    for i in range(per):
+        for c in tok_copies(i):
+            c.wait_send()
     for c in (out_y, out_core, out_on, *tok_on):
         c.wait_send()
     for c in written:
@@ -1321,7 +1322,7 @@
     )
     tok_v, out_v, up_v, dn_v, kv_v, tok_w, up_w, dn_w, ow_w, qkv_w, sem_in, sem_out = refs
     D, L, hidden, T = plan.D, plan.L, plan.F, plan.T
-    pieces = 4
+    pieces = 8
     size = T // pieces
     reads = [
         pltpu.make_async_copy(a, b, sem_in.at[i])
@@ -1346,12 +1347,16 @@
 
     for i in range(pieces):
         token_reads[i].wait()
+        if i == 1:
+            reads[3].wait()
+            for part in range(2):
+                through = pl.ds(part * (T // 2), T // 2)
+                send(out_v.at[through], out_o.at[through])
         rows = pl.ds(i * size, size)
         tok_w[rows, :] = tok_v[rows, :].astype(F32)
         send(tok_w.at[rows], tok_o.at[rows])
-    for c in reads:
+    for c in reads[:3]:
         c.wait()
-    send(out_v, out_o)
     up_w[...] = up_v[...].astype(F32)
     send(up_w, up_o)
     dn_w[...] = dn_v[0:hidden, :].astype(F32)
@@ -1402,8 +1407,8 @@
             pltpu.VMEM((hidden, D), F32),
             pltpu.VMEM((L, D), F32),
             pltpu.VMEM((3, D, L), F32),
-            pltpu.SemaphoreType.DMA((8,)),
             pltpu.SemaphoreType.DMA((16,)),
+            pltpu.SemaphoreType.DMA((24,)),
         ],
         compiler_params=pltpu.CompilerParams(vmem_limit_bytes=60 << 20),
         name="widen",

time: 168 us -> 164 us (0.976); the launches traced: 166 us -> 164 us
  Pallas kernels: 165 us -> 163 us
    pallas_call x1, Pallas kernels: 157 us -> 155 us  [per_device(): pl.pallas_call(functools.partial(layer_kernel, plan), out_shape=[jax.Shap...]
where the time goes in v1:
time: 164 us
  Pallas kernels  163 us (99%)
    pallas_call x1, Pallas kernels, per_device(): pl.pallas_call(functools.partial(layer_kernel, plan), out_shape=[jax.Shap...  155 us
    pallas_call x1, Pallas kernels, widen(): pl.pallas_call(functools.partial(widen_kernel, plan), out_shape=[jax.Shap...  8.03 us

profile of v1, /device:TPU:12, one launch (start us, length us, event | category | flops | bytes accessed | tf_op | source)
XLA Modules:
  0.0 163.6 jit_solution(12187557269997426741)
XLA Ops:
  0.7 154.8 %performer_layer.1 = (bf16[2048,512]{1,0:T(8,128)(2,1)}, bf16[2048,512]{1,0:T(8,128)(2,1)}, bf16[512,512]{1,0:T(8,128)(2,1)}, bf16[768,512]{1,0:T(8,128)(2,1)}, ...) custom-call(bf16[2048,512]{1,0:T(8,128)(2,1)} %refs_0_.1, s32[16,128]{1,0:T(8,128)} %bitcast.16, s32[16,128]{1,0:T(8,128)} %bitcast.17, ...), custom_call_target="tpu_custom_call" | custom-call | tf_op jit(solution)/shard_map/performer_layer/pallas_call | solution.py:1445
  155.4 8.0 %widen.1 = (bf16[2048,512]{1,0:T(8,128)(2,1)}, f32[2048,512]{1,0:T(8,128)}, f32[3,512,128]{2,1,0:T(8,128)}, f32[128,512]{1,0:T(8,128)}, f32[1,512]{1,0:T(1,128)}...) custom-call(bf16[2048,512]{1,0:T(8,128)(2,1)} %get-tuple-element.32., ...), custom_call_target="tpu_custom_call" | custom-call | tf_op jit(solution)/shard_map/widen/pallas_call | solution.py:1392

commit v2 on v1

--- a/solution.py
+++ b/solution.py
@@ -782,18 +782,26 @@
 
     r.small[...] = jnp.zeros((16, D), F32)
 
-    def units(rows, s):
-        up, down = r.up_g[s], r.dn_g[s]
-        preact = dot(r.nm2[rows, :], up) + r.ub_g[s]
-        spread = 0.5 + 0.5 * lax.erf(preact * (0.5**0.5))
-        active = (preact * spread).astype(BF)
-        r.act[s, rows, :] = active
-        slope = spread + preact * jnp.exp(preact * preact * -0.5) * 0.3989422804014327
-        grad = (dot_nt(r.cotv[rows, :], down) * slope).astype(BF)
-        r.gp[s, rows, :] = grad
-        r.bo[...] += dot(active, down)
-        r.gn2[...] += dot_nt(grad, up)
-        r.small[pl.ds(8 + s, 1), :] += jnp.sum(grad.astype(F32), 0, keepdims=True)
+    beside = 1 if plan.big else 2
+
+    def units(rows, group):
+        both = [beside * group + i for i in range(beside)]
+        normed, cotangent = r.nm2[rows, :], r.cotv[rows, :]
+        preacts = [dot(normed, r.up_g[s]) + r.ub_g[s] for s in both]
+        backs = [dot_nt(cotangent, r.dn_g[s]) for s in both]
+        forward, backward = r.bo[...], r.gn2[...]
+        for s, preact, back in zip(both, preacts, backs, strict=True):
+            spread = 0.5 + 0.5 * lax.erf(preact * (0.5**0.5))
+            active = (preact * spread).astype(BF)
+            r.act[s, rows, :] = active
+            slope = spread + preact * jnp.exp(preact * preact * -0.5) * 0.3989422804014327
+            grad = (back * slope).astype(BF)
+            r.gp[s, rows, :] = grad
+            forward += dot(active, r.dn_g[s])
+            backward += dot_nt(grad, r.up_g[s])
+            r.small[pl.ds(8 + s, 1), :] += jnp.sum(grad.astype(F32), 0, keepdims=True)
+        r.bo[...] = forward
+        r.gn2[...] = backward
 
     gas = r.attb.reshape(nm, Tm, L)
 
@@ -815,7 +823,7 @@
         r.nm2[rows, :] = normed.astype(BF)
         r.bo[...] = jnp.zeros((TILE, D), F32)
         r.gn2[...] = jnp.zeros((TILE, D), F32)
-        lax.fori_loop(0, nm, lambda s, carry: (units(rows, s), carry)[1], 0)
+        lax.fori_loop(0, nm // beside, lambda s, carry: (units(rows, s), carry)[1], 0)
         middle = r.mid[rows, :]
         r.outv[rows, :] = (middle + r.bo[...] + r.db[...]).astype(BF)
         hat, scale = normalised(middle)
@@ -1142,8 +1150,6 @@
         small_scatter()
 
     second.run(in_quarters(query_back, wide), after_queries, early_keys, midway)
-    dn.scatter()
-    out_land[mine, :] = r.outv[...]
 
     def key_back(i):
         rows = rows_of(i, TILE)
@@ -1165,7 +1171,12 @@
             i,
         )
 
-    each_tile(key_back, key_copy, up.gather)
+    def between_halves():
+        up.gather()
+        dn.scatter()
+        out_land[mine, :] = r.outv[...]
+
+    each_tile(key_back, key_copy, between_halves)
     for a in range(3):
         r.garr[m, a] = r.grads[a, rows_of(m, Tm), :]
 

time: 164 us -> 162 us (0.988)
  Pallas kernels: 163 us -> 161 us
where the time goes in v2:
time: 162 us
  Pallas kernels  161 us (99%)
    pallas_call x1, Pallas kernels, per_device(): pl.pallas_call(functools.partial(layer_kernel, plan), out_shape=[jax.Shap...  153 us
    pallas_call x1, Pallas kernels, widen(): pl.pallas_call(functools.partial(widen_kernel, plan), out_shape=[jax.Shap...  8.03 us

profile of v2, /device:TPU:12, one launch (start us, length us, event | category | flops | bytes accessed | tf_op | source)
XLA Modules:
  0.0 162.0 jit_solution(15722706036826752526)
XLA Ops:
  0.7 153.2 %performer_layer.1 = (bf16[2048,512]{1,0:T(8,128)(2,1)}, bf16[2048,512]{1,0:T(8,128)(2,1)}, bf16[512,512]{1,0:T(8,128)(2,1)}, bf16[768,512]{1,0:T(8,128)(2,1)}, ...) custom-call(bf16[2048,512]{1,0:T(8,128)(2,1)} %refs_0_.1, s32[16,128]{1,0:T(8,128)} %bitcast.16, s32[16,128]{1,0:T(8,128)} %bitcast.17, ...), custom_call_target="tpu_custom_call" | custom-call | tf_op jit(solution)/shard_map/performer_layer/pallas_call | solution.py:1456
  153.8 8.0 %widen.1 = (bf16[2048,512]{1,0:T(8,128)(2,1)}, f32[2048,512]{1,0:T(8,128)}, f32[3,512,128]{2,1,0:T(8,128)}, f32[128,512]{1,0:T(8,128)}, f32[1,512]{1,0:T(1,128)}...) custom-call(bf16[2048,512]{1,0:T(8,128)(2,1)} %get-tuple-element.32., ...), custom_call_target="tpu_custom_call" | custom-call | tf_op jit(solution)/shard_map/widen/pallas_call | solution.py:1403

commit v3 on v2

--- a/solution.py
+++ b/solution.py
@@ -1136,10 +1136,10 @@
         up.start()
 
     def midway():
+        out_y.start()
+        out_core.start()
         y_sum(dn_y, r.dnp, r.dnc, r.dny)
         dn.start()
-        out_y.start()
-        out_core.start()
         up.scatter()
 
     def after_queries():

time: 162 us -> 162 us (level)
  no operation moved by 1% of the time
where the time goes in v3:
time: 162 us
  Pallas kernels  161 us (99%)
    pallas_call x1, Pallas kernels, per_device(): pl.pallas_call(functools.partial(layer_kernel, plan), out_shape=[jax.Shap...  153 us
    pallas_call x1, Pallas kernels, widen(): pl.pallas_call(functools.partial(widen_kernel, plan), out_shape=[jax.Shap...  8.03 us

profile of v3, /device:TPU:12, one launch (start us, length us, event | category | flops | bytes accessed | tf_op | source)
XLA Modules:
  0.0 162.0 jit_solution(11121147934413016804)
XLA Ops:
  0.7 153.2 %performer_layer.1 = (bf16[2048,512]{1,0:T(8,128)(2,1)}, bf16[2048,512]{1,0:T(8,128)(2,1)}, bf16[512,512]{1,0:T(8,128)(2,1)}, bf16[768,512]{1,0:T(8,128)(2,1)}, ...) custom-call(bf16[2048,512]{1,0:T(8,128)(2,1)} %refs_0_.1, s32[16,128]{1,0:T(8,128)} %bitcast.16, s32[16,128]{1,0:T(8,128)} %bitcast.17, ...), custom_call_target="tpu_custom_call" | custom-call | tf_op jit(solution)/shard_map/performer_layer/pallas_call | solution.py:1456
  153.8 8.0 %widen.1 = (bf16[2048,512]{1,0:T(8,128)(2,1)}, f32[2048,512]{1,0:T(8,128)}, f32[3,512,128]{2,1,0:T(8,128)}, f32[128,512]{1,0:T(8,128)}, f32[1,512]{1,0:T(1,128)}...) custom-call(bf16[2048,512]{1,0:T(8,128)(2,1)} %get-tuple-element.32., ...), custom_call_target="tpu_custom_call" | custom-call | tf_op jit(solution)/shard_map/widen/pallas_call | solution.py:1403
